TPU v7x, 256 devices: a whole 4x4x8 slice. The times are simulated.
256 devices in a mesh: song: 4 (over y), seq: 64 (over z, x, core).
Axes of the slice: x: 4, y: 4, z: 8, core: 2. Of those that a mesh axis runs over, the one named last changes fastest.
Arguments:
- queries: bfloat16 [4, 8192, 2048], P('song', 'seq'), may hold values from -64 to 64
- keys: bfloat16 [4, 8192, 2048], P('song', 'seq'), may hold values from -64 to 64
- values: bfloat16 [4, 8192, 2048], P('song', 'seq'), may hold values from -6 to 6
- lyric_keys: bfloat16 [4, 384, 2048], P('song', 'seq'), may hold values from -64 to 64
- lyric_values: bfloat16 [4, 384, 2048], P('song', 'seq'), may hold values from -6 to 6
- q_gain: float32 [128], replicated, may hold values from 0.5 to 1.5
- k_gain: float32 [128], replicated, may hold values from 0.5 to 1.5
- cotangent: bfloat16 [4, 8192, 2048], P('song', 'seq'), may hold values from -12 to 12
- alignment: int32 [4, 64, 2], P('song', 'seq'), may hold values from -1 to 2, as said below
- lyric_len: int32 [4], P('song'), may hold values from 192 to 384
Outputs:
- attn_out: bfloat16 [4, 8192, 2048], P('song', 'seq')
- grad_queries: bfloat16 [4, 8192, 2048], P('song', 'seq')
- grad_keys: bfloat16 [4, 8192, 2048], P('song', 'seq')
- grad_values: bfloat16 [4, 8192, 2048], P('song', 'seq')
- grad_lyric_keys: bfloat16 [4, 384, 2048], P('song', 'seq')
- grad_lyric_values: bfloat16 [4, 384, 2048], P('song', 'seq')
- grad_q_gain: float32 [128], replicated
- grad_k_gain: float32 [128], replicated
Inputs may be any that keep to these rules, and one draw needn't show every extreme that they name: `alignment`: in each row the entries that are not -1 are distinct.
All inputs are finite; a program needn't handle non-finite values.
Results may differ from a plain program's by a relative error of at most 0.01.
Values may be sent and summed in bfloat16 or wider, within the bound.
A program may use at most 128 MiB of HBM per device.

v0:
```python
import jax
import jax.numpy as jnp
from jax import lax
from jax.sharding import PartitionSpec as P

BLK = 128
WIN = 1
TILES = 2
NORM_EPS = 1e-06


def extended_2(block, sides, width):
    for axis, dim in sides:
        count = lax.axis_size(axis)
        forward = [(i, i + 1) for i in range(count - 1)]
        backward = [(target, source) for source, target in forward]
        low = lax.ppermute(
            lax.slice_in_dim(block, block.shape[dim] - width, None, axis=dim), axis, forward
        )
        high = lax.ppermute(lax.slice_in_dim(block, 0, width, axis=dim), axis, backward)
        block = jnp.concatenate([low, block, high], axis=dim)
    return block


def norm_heads(inputs, norm_gain):
    row_values = inputs.astype(jnp.float32).reshape(inputs.shape[0], -1, norm_gain.shape[0])
    inverse = lax.rsqrt(jnp.mean(row_values * row_values, axis=-1, keepdims=True) + NORM_EPS)
    return (row_values * inverse * norm_gain, inverse)


def norm_back(inputs, inverse, norm_gain, grad_out):
    row_values = inputs.astype(jnp.float32).reshape(grad_out.shape)
    scaled = grad_out * norm_gain
    grad_input = inverse * scaled - row_values * inverse * inverse * inverse * jnp.mean(
        scaled * row_values, axis=-1, keepdims=True
    )
    grad_gain = jnp.sum(grad_out * row_values * inverse, axis=(0, 1))
    return (grad_input.reshape(inputs.shape), grad_gain)


def block_pass(query_rows, key_rows, value_rows, keep_mask, grad_rows, score_scale):
    scores = (
        jnp.einsum("qhd,khd->hqk", query_rows, key_rows, preferred_element_type=jnp.float32)
        * score_scale
    )
    exp_scores = jnp.where(keep_mask[None, None, :], jnp.exp(scores), 0.0)
    totals = jnp.sum(exp_scores, axis=2)
    prob_full = exp_scores / totals[:, :, None]
    prob_low = prob_full.astype(jnp.bfloat16)
    block_output = jnp.einsum(
        "hqk,khd->qhd", prob_low, value_rows, preferred_element_type=jnp.float32
    ).astype(jnp.bfloat16)
    delta_rows = jnp.sum(grad_rows.astype(jnp.float32) * block_output.astype(jnp.float32), axis=2).T
    grad_prob = jnp.einsum(
        "qhd,khd->hqk", grad_rows, value_rows, preferred_element_type=jnp.float32
    )
    grad_score = (prob_full * (grad_prob - delta_rows[:, :, None])).astype(jnp.bfloat16)
    query_gradient = (
        jnp.einsum("hqk,khd->qhd", grad_score, key_rows, preferred_element_type=jnp.float32)
        * score_scale
    )
    grad_key = (
        jnp.einsum("hqk,qhd->khd", grad_score, query_rows, preferred_element_type=jnp.float32)
        * score_scale
    )
    value_gradient = jnp.einsum(
        "hqk,qhd->khd", prob_low, grad_rows, preferred_element_type=jnp.float32
    )
    return (block_output, query_gradient, grad_key, value_gradient, totals, delta_rows)


def body(
    queries, keys, values, lyric_keys, lyric_values, q_gain, k_gain, cotangent, alignment, lyric_len
):
    head_size = q_gain.shape[0]
    model_width = queries.shape[2]
    head_count = model_width // head_size
    frames = queries.shape[1]
    lyric_local = lyric_keys.shape[1]
    blocks = frames // BLK
    border_rows = WIN * BLK
    window_extent = (2 * WIN + 1) * BLK
    score_scale = head_size ** (-0.5)
    total_frames = frames * lax.axis_size("seq")
    first_frame = lax.axis_index("seq") * frames
    query_raw = queries[0]
    key_raw = keys[0]
    query_full, query_inv = norm_heads(query_raw, q_gain)
    key_full, key_inv = norm_heads(key_raw, k_gain)
    lyric_full, lyric_inv = norm_heads(lyric_keys[0], k_gain)
    query_norm = query_full.astype(jnp.bfloat16)
    key_norm = key_full.astype(jnp.bfloat16)
    lyric_norm = lyric_full.astype(jnp.bfloat16)
    lyric_key_all, lyric_val_all = (
        lax.all_gather(lyric_norm.reshape(lyric_local, model_width), "seq", axis=0, tiled=True),
        lax.all_gather(lyric_values[0], "seq", axis=0, tiled=True),
    )
    lyric_total = lyric_key_all.shape[0]
    lyric_key_all = lyric_key_all.reshape(lyric_total, head_count, head_size)
    lyric_val_all = lyric_val_all.reshape(lyric_total, head_count, head_size)
    stacked = jnp.stack([key_norm.reshape(frames, model_width), values[0]])
    extended = extended_2(stacked, (("seq", 1),), border_rows)
    ext_keys = extended[0].reshape(frames + 2 * border_rows, head_count, head_size)
    ext_vals = extended[1].reshape(frames + 2 * border_rows, head_count, head_size)
    grad_heads = cotangent[0].reshape(frames, head_count, head_size)
    length = lyric_len[0]

    def one_block(block_id):
        start_offset = block_id * BLK
        position = (
            first_frame + start_offset - border_rows + jnp.arange(window_extent, dtype=jnp.int32)
        )
        audio_mask = (position >= 0) & (position < total_frames)
        tile_ids = alignment[0, block_id]
        row_grid = (jnp.maximum(tile_ids, 0) * BLK)[:, None] + jnp.arange(BLK, dtype=jnp.int32)[
            None, :
        ]
        lyric_mask = ((tile_ids >= 0)[:, None] & (row_grid < length)).reshape(-1)
        row_index = row_grid.reshape(-1)
        all_keys = jnp.concatenate([ext_keys, jnp.take(lyric_key_all, row_index, axis=0)], axis=0)
        all_vals = jnp.concatenate([ext_vals, jnp.take(lyric_val_all, row_index, axis=0)], axis=0)
        keep_mask = jnp.concatenate([audio_mask, lyric_mask], axis=0)
        results = block_pass(query_norm, all_keys, all_vals, keep_mask, grad_heads, score_scale)
        return results + (row_index,)

    output_list, grad_qn, grad_key, value_gradient, totals, delta_rows, row_index = lax.map(
        one_block, jnp.arange(blocks, dtype=jnp.int32)
    )
    audio_cols = grad_key.shape[1] - TILES * BLK
    flat_rows = row_index.reshape(-1)
    lyric_grad_key = (
        jnp.zeros((lyric_total, head_count, head_size), jnp.float32)
        .at[flat_rows]
        .add(grad_key[:, audio_cols:].reshape(-1, head_count, head_size))
    )
    lyric_grad_val = (
        jnp.zeros((lyric_total, head_count, head_size), jnp.float32)
        .at[flat_rows]
        .add(value_gradient[:, audio_cols:].reshape(-1, head_count, head_size))
    )
    ext_grad_key = jnp.zeros((frames + 2 * border_rows, head_count, head_size), jnp.float32)
    ext_grad_val = jnp.zeros((frames + 2 * border_rows, head_count, head_size), jnp.float32)
    block_id = 0
    lower = block_id * BLK
    ext_grad_key = ext_grad_key.at[lower : lower + window_extent].add(
        grad_key[block_id, :window_extent]
    )
    ext_grad_val = ext_grad_val.at[lower : lower + window_extent].add(
        value_gradient[block_id, :window_extent]
    )
    own_grad_key = ext_grad_key[border_rows : border_rows + frames]
    own_grad_val = ext_grad_val[border_rows : border_rows + frames]
    rims = jnp.stack(
        [
            jnp.concatenate(
                [ext_grad_key[:border_rows], ext_grad_key[border_rows + frames :]], axis=0
            ).reshape(2 * border_rows, model_width),
            jnp.concatenate(
                [ext_grad_val[:border_rows], ext_grad_val[border_rows + frames :]], axis=0
            ).reshape(2 * border_rows, model_width),
        ]
    )
    received = extended_2(rims.astype(jnp.bfloat16), (("seq", 1),), border_rows).astype(rims.dtype)
    from_left = received[:, :border_rows].reshape(2, border_rows, head_count, head_size)
    from_right = received[:, 3 * border_rows :].reshape(2, border_rows, head_count, head_size)
    own_grad_key = (
        own_grad_key.at[:border_rows]
        .add(from_left[0])
        .at[frames - border_rows :]
        .add(from_right[0])
    )
    own_grad_val = (
        own_grad_val.at[:border_rows]
        .add(from_left[1])
        .at[frames - border_rows :]
        .add(from_right[1])
    )
    unnormed_query_gradient, query_gain_vector = norm_back(
        query_raw, query_inv, q_gain, grad_qn.reshape(frames, head_count, head_size)
    )
    unnormed_key_gradient, key_gain_vector = norm_back(key_raw, key_inv, k_gain, own_grad_key)
    summed_key, summed_val = (
        lax.psum_scatter(
            lyric_grad_key.reshape(lyric_total, model_width), "seq", scatter_dimension=0, tiled=True
        ),
        lax.psum_scatter(
            lyric_grad_val.reshape(lyric_total, model_width), "seq", scatter_dimension=0, tiled=True
        ),
    )
    unnormed_lyric_gradient, lyric_gain_vector = norm_back(
        lyric_keys[0], lyric_inv, k_gain, summed_key.reshape(lyric_local, head_count, head_size)
    )
    total_query_gain, total_key_gain = lax.psum(
        (query_gain_vector, key_gain_vector + lyric_gain_vector), ("song", "seq")
    )
    return (
        output_list.reshape(1, frames, model_width),
        unnormed_query_gradient.astype(jnp.bfloat16)[None],
        unnormed_key_gradient.astype(jnp.bfloat16)[None],
        own_grad_val.reshape(1, frames, model_width).astype(jnp.bfloat16),
        unnormed_lyric_gradient.astype(jnp.bfloat16)[None],
        summed_val.astype(jnp.bfloat16)[None],
        total_query_gain,
        total_key_gain,
    )


def solution(mesh):
    in_specs = (
        P("song", "seq", None),
        P("song", "seq", None),
        P("song", "seq", None),
        P("song", "seq", None),
        P("song", "seq", None),
        P(),
        P(),
        P("song", "seq", None),
        P("song", "seq", None),
        P("song"),
    )
    out_specs = (
        P("song", "seq", None),
        P("song", "seq", None),
        P("song", "seq", None),
        P("song", "seq", None),
        P("song", "seq", None),
        P("song", "seq", None),
        P(),
        P(),
    )
    return jax.shard_map(body, mesh=mesh, in_specs=in_specs, out_specs=out_specs, check_vma=False)
```

profile of v0, /device:TPU:1, one launch (start us, length us, event | category | flops | bytes accessed | tf_op | source)
XLA Modules:
  0.0 654.3 jit_solution(4677205366677550377)
XLA Ops:
  7.2 1.4 copy.99
  8.7 0.8 convert_bitcast_fusion
  9.6 0.7 broadcast_bitcast_fusion.2
  10.3 1.4 fusion.41
  11.8 1.3 copy.98
  13.1 1.4 copy.97
  14.5 1.2 multiply_reduce_fusion.2
  15.7 0.4 multiply_convert_fusion.1
  16.2 5.2 collective-permute-start.1
  21.4 1.9 collective-permute-start
  24.1 1.0 copy.107
  25.1 1.2 copy.103
  26.4 0.7 dynamic-slice.30
  27.9 5.7 collective-permute-done.1
  33.6 1.9 collective-permute-done
  35.5 1.7 pad_maximum_fusion
  37.3 1.5 fusion.52
  38.8 1.6 copy.105
  40.4 53.5 %all-gather.5.cloned.1.call-done = bf16[1,384,2048]{2,0,1:T(2,128)(2,1)} async-done(((bf16[1,6,2048]{2,0,1:T(2,128)(2,1)}), bf16[1,384,2048]{2,0,1:T(2,128)(2,1)}) %all-gather.5.cloned.1.call-update) | async-done | bytes 1572880 | tf_op jit(solution)/shard_map/all_gather | solution.py:96
  93.9 6.9 %copy.100 = bf16[1,384,2048]{1,2,0:T(8,128)(2,1)S(1)} copy(bf16[1,384,2048]{2,0,1:T(2,128)(2,1)} %all-gather.5.cloned.1.call-done) | data formatting | bytes 3145728 | tf_op jit(solution)/shard_map/all_gather | solution.py:96
  100.9 2.0 copy.101
  102.9 69.1 %all-gather.7.cloned.1.call-done = bf16[64,6,2048]{2,1,0:T(8,128)(2,1)} async-done(((bf16[1,6,2048]{2,1,0:T(8,128)(2,1)}), bf16[64,6,2048]{2,1,0:T(8,128)(2,1)}) %all-gather.7.cloned.1.call-update) | async-done | bytes 1572880 | tf_op jit(solution)/shard_map/all_gather | solution.py:95
  172.0 4.4 reshape.472
  176.4 3.2 gather_fusion.1
  179.6 1.8 gather_fusion
  181.3 1.6 copy.102
  183.0 1.6 copy_select_fusion
  184.7 1.6 fusion.2
  186.3 3.1 fusion.56
  189.5 2.4 multiply_reduce_fusion
  191.9 1.8 fusion
  193.7 0.9 fusion.57
  194.6 0.6 copy-done.14
  195.3 0.3 fusion.54
  195.8 0.3 maximum_maximum_fusion
  196.1 0.5 copy-done.5
  196.8 2.1 fusion.55
  198.9 2.1 collective-permute-start.3
  201.0 3.6 collective-permute-start.2
  204.8 2.0 copy.112
  206.8 0.2 broadcast.403.clone
  207.0 20.2 %scatter_fusion = f32[384,16,128]{2,1,0:T(8,128)S(1)} fusion(f32[384,16,128]{2,1,0:T(8,128)S(1)} %broadcast.403.clone, s32[256]{0:T(256)S(1)} %bitcast.227, f32[256,16,128]{2,1,0:T(8,128)} %copy.112), kind=kCustom, calls=%fused_computation.2 | custom fusion | flops 524288 | bytes 6292480 | tf_op jit(solution)/shard_map/scatter-add | solution.py:134
  227.3 3.1 copy.146
  230.3 1.8 slice_bitcast_fusion
  232.1 2.0 copy.113
  234.4 20.2 %scatter_fusion.1 = f32[384,16,128]{2,1,0:T(8,128)S(1)} fusion(f32[384,16,128]{2,1,0:T(8,128)S(1)} %broadcast.403.clone.1, s32[256]{0:T(256)S(1)} %bitcast.228, f32[256,16,128]{2,1,0:T(8,128)} %copy.113), kind=kCustom, calls=%fused_computation.3 | custom fusion | flops 524288 | bytes 6292480 | tf_op jit(solution)/shard_map/scatter-add | solution.py:139
  254.6 3.1 copy.145
  257.7 279.7 %all-reduce.7 = bf16[384,2048]{1,0:T(8,128)(2,1)} all-reduce(f32[384,2048]{1,0:T(8,128)} %bitcast.203), channel_id=4, replica_groups=mesh['song'=4,'seq'=64] {'seq'}, use_global_device_ids=true, to_apply=%region_11.13.clone | all-reduce | flops 786432 | bytes 4718592
  537.4 4.1 fusion.18
  541.6 1.3 slice.221
  542.9 2.4 slice.228
  545.3 2.0 copy.114
  547.4 2.3 fusion.25
  549.7 2.0 copy.115
  551.7 1.5 fusion.40
  553.2 1.8 fusion.14
  555.0 1.6 fusion.22
  556.7 1.2 fusion.12
  557.9 2.0 copy.116
  559.9 1.7 fusion.16
  561.6 1.0 copy.117
  562.7 0.9 dynamic-slice_bitcast_fusion
  563.8 1.6 fusion.33
  565.4 82.4 %all-reduce.2 = (f32[128]{0:T(128)}, f32[128]{0:T(128)}) all-reduce(f32[128]{0:T(128)S(1)} %get-tuple-element.214, f32[128]{0:T(128)S(1)} %add.202), channel_id=1, replica_groups=mesh['song'=4,'seq'=64] {'song','seq'}, use_global_device_ids=true, to_apply=%region_13.15 | all-reduce | flops 256 | bytes 2048 | tf_op jit(solution)/shard_map/psum | solution.py:193
  (86 shorter events, 1.9 us)
Async XLA Ops:
  7.2 86.8 %all-gather.5.cloned.1.call-start = ((), (), s32[]{:S(2)}) async-start(), calls=%async_computation | async-start | bytes 3194880 | tf_op jit(solution)/shard_map/all_gather | solution.py:96
  8.7 163.3 %all-gather.7.cloned.1.call-start = ((), (), s32[]{:S(2)}) async-start(), calls=%async_computation.1 | async-start | bytes 2129920 | tf_op jit(solution)/shard_map/all_gather | solution.py:95
  11.7 550.9 %all-reduce.6.cloned.1.call-start = ((), (), s32[]{:S(2)}) async-start(), calls=%async_computation.2 | async-start | bytes 6291456
  13.1 10.9 %copy-start.24 = (s32[1,1,2]{2,1,0:T(1,128)S(1)}, s32[1,1,2]{2,1,0:T(1,128)}, u32[]{:S(2)}) copy-start(s32[1,1,2]{2,1,0:T(1,128)} %param.44) | copy-start | bytes 28
  13.1 11.0 %copy-start.19 = (bf16[1,128,2048]{2,1,0:T(8,128)(2,1)S(1)}, bf16[1,128,2048]{2,1,0:T(8,128)(2,1)}, u32[]{:S(2)}) copy-start(bf16[1,128,2048]{2,1,0:T(8,128)(2,1)} %param.43) | copy-start | bytes 1572868
  14.5 9.6 %copy-start.3 = (bf16[1,128,2048]{1,2,0:T(8,128)(2,1)}, bf16[1,128,2048]{1,2,0:T(8,128)(2,1)S(1)}, u32[]{:S(2)}) copy-start(bf16[1,128,2048]{1,2,0:T(8,128)(2,1)S(1)} %copy.97) | copy-start | bytes 1572868
  15.7 10.7 %copy-start.25 = (u32[256]{0:T(256)S(1)}, u32[256]{0:T(256)}, u32[]{:S(2)}) copy-start(u32[256]{0:T(256)} %constant.274) | copy-start | bytes 3076
  16.1 11.7 %copy-start.23 = (f32[128]{0:T(128)S(1)}, f32[128]{0:T(128)}, u32[]{:S(2)}) copy-start(f32[128]{0:T(128)} %param.41) | copy-start | bytes 1540
  16.2 17.4 %collective-permute-start.1 = (bf16[2,128,2048]{1,2,0:T(8,128)(2,1)S(1)}, bf16[2,128,2048]{1,2,0:T(8,128)(2,1)}, u32[]{:S(2)}, u32[]{:S(2)}) collective-permute-start(bf16[2,128,2048]{1,2,0:T(8,128)(2,1)S(1)} %pad_maximum_fusion.9), channel_id=1, source_target_pairs={{1,0},{2,1},{3,2},{4,3},{5,4},{6,5},{7,6},{8,7},{9,8},{10,9},{11,1... | collective-permute-start | bytes 3145736 | tf_op jit(solution)/shard_map/ppermute | solution.py:20
  21.4 14.2 %collective-permute-start = (bf16[2,128,2048]{1,2,0:T(8,128)(2,1)S(1)}, bf16[2,128,2048]{1,2,0:T(8,128)(2,1)}, u32[]{:S(2)}, u32[]{:S(2)}) collective-permute-start(bf16[2,128,2048]{1,2,0:T(8,128)(2,1)S(1)} %pad_maximum_fusion.9), channel_id=1, source_target_pairs={{0,1},{1,2},{2,3},{3,4},{4,5},{5,6},{6,7},{7,8},{8,9},{9,10},{10,1... | collective-permute-start | bytes 3145736 | tf_op jit(solution)/shard_map/ppermute | solution.py:17
  26.4 167.4 %copy-start.1 = (f32[1,128,2048]{1,2,0:T(8,128)}, f32[1,128,2048]{1,2,0:T(8,128)S(1)}, u32[]{:S(2)}) copy-start(f32[1,128,2048]{1,2,0:T(8,128)S(1)} %copy.103) | copy-start | bytes 3145732
  102.9 76.7 %copy-start.12 = (bf16[384,16,128]{2,1,0:T(8,128)(2,1)S(1)}, bf16[384,16,128]{2,1,0:T(8,128)(2,1)}, u32[]{:S(2)}) copy-start(bf16[384,16,128]{2,1,0:T(8,128)(2,1)} %copy.101) | copy-start | bytes 4718596
  183.0 1.8 copy-start.15
  184.6 1.7 copy-start.18
  184.7 1.6 copy-start.20
  186.3 3.1 copy-start.17
  193.7 1.5 copy-start.14
  195.3 9.4 %copy-start = (f32[1,640,16,128]{1,3,2,0:T(8,128)}, f32[1,640,16,128]{1,3,2,0:T(8,128)S(1)}, u32[]{:S(2)}) copy-start(f32[1,640,16,128]{1,3,2,0:T(8,128)S(1)} %get-tuple-element.244) | copy-start | bytes 15728644
  195.6 1.0 copy-start.5
  195.6 1.2 copy-start.7
  195.8 3.1 copy-start.9
  195.8 3.1 copy-start.11
  198.9 354.3 %collective-permute-start.3 = (bf16[2,128,2048]{1,2,0:T(8,128)(2,1)}, bf16[2,128,2048]{1,2,0:T(8,128)(2,1)}, u32[]{:S(2)}, u32[]{:S(2)}) collective-permute-start(bf16[2,128,2048]{1,2,0:T(8,128)(2,1)} %get-tuple-element.234), channel_id=1, source_target_pairs={{1,0},{2,1},{3,2},{4,3},{5,4},{6,5},{7,6},{8,7},{9,8},{10,9},{11,1... | collective-permute-start | bytes 3145736 | tf_op jit(solution)/shard_map/ppermute | solution.py:20
  201.0 352.2 %collective-permute-start.2 = (bf16[2,128,2048]{1,2,0:T(8,128)(2,1)}, bf16[2,128,2048]{1,2,0:T(8,128)(2,1)}, u32[]{:S(2)}, u32[]{:S(2)}) collective-permute-start(bf16[2,128,2048]{1,2,0:T(8,128)(2,1)} %get-tuple-element.233), channel_id=1, source_target_pairs={{0,1},{1,2},{2,3},{3,4},{4,5},{5,6},{6,7},{7,8},{8,9},{9,10},{10,1... | collective-permute-start | bytes 3145736 | tf_op jit(solution)/shard_map/ppermute | solution.py:17
  257.7 279.7 %copy-start.2 = (f32[1,128,2048]{1,2,0:T(8,128)S(1)}, f32[1,128,2048]{1,2,0:T(8,128)}, u32[]{:S(2)}) copy-start(f32[1,128,2048]{1,2,0:T(8,128)} %copy-done.1) | copy-start | bytes 3145732
  257.7 279.7 %copy-start.16 = (bf16[384,16,128]{2,0,1:T(8,128)(2,1)S(1)}, bf16[384,16,128]{2,0,1:T(8,128)(2,1)}, u32[]{:S(2)}) copy-start(bf16[384,16,128]{2,0,1:T(8,128)(2,1)} %copy.105) | copy-start | bytes 4718596
  542.9 10.3 %copy-start.4 = (bf16[1,128,2048]{1,2,0:T(8,128)(2,1)S(1)}, bf16[1,128,2048]{1,2,0:T(8,128)(2,1)}, u32[]{:S(2)}) copy-start(bf16[1,128,2048]{1,2,0:T(8,128)(2,1)} %copy-done.3) | copy-start | bytes 1572868
  542.9 10.3 %copy-start.6 = (bf16[1,128,16,128]{1,3,2,0:T(8,128)(2,1)S(1)}, bf16[1,128,16,128]{1,3,2,0:T(8,128)(2,1)}, u32[]{:S(2)}) copy-start(bf16[1,128,16,128]{1,3,2,0:T(8,128)(2,1)} %copy-done.5) | copy-start | bytes 1572868
  553.2 1.8 copy-start.13
  553.2 1.8 copy-start.22
  556.6 3.3 copy-start.8
  556.6 3.3 copy-start.10
  559.9 3.8 copy-start.21
Sparse Core Ops, SparseCore 0:
  11.3 82.5 all-gather.4
  97.3 74.6 all-gather.6
  230.5 192.0 all-reduce.5
where the time goes:
time: 656 us; the launch traced here: 654 us
  blocking collectives  362 us (55%)
  waiting for transfers between devices  130 us (20%)
  local copies, waits for them, and re-layouts  60.6 us (9%)
  other arithmetic  58.7 us (9%)
  between operations  15.6 us (2%)
  matrix products  14 us (2%)
  starting transfers between devices  12.9 us (2%)
    unnamed x1, blocking collectives  280 us
    psum x1, blocking collectives, body(): lax.psum((query_gain_vector, key_gain_vector + lyric_gain_vector), ('song...  82.4 us
    all_gather x1, waiting for transfers between devices, body(): lax.all_gather(lyric_norm.reshape(lyric_local, model_width), 'seq', axis=...  69.1 us
    all_gather x1, waiting for transfers between devices, body(): lax.all_gather(lyric_values[0], 'seq', axis=0, tiled=True)  53.5 us
    unnamed x66, local copies, waits for them, and re-layouts  21.5 us
    scatter-add x1, other arithmetic, body(): lyric_grad_val = jnp.zeros((lyric_total, head_count, head_size), jnp.floa...  20.2 us
    scatter-add x1, other arithmetic, body(): lyric_grad_key = jnp.zeros((lyric_total, head_count, head_size), jnp.floa...  20.2 us
  transfers between devices with their start and end apart: 7, of which 4 were waited for; matrix products, arithmetic and copies ran while one was open for 16% of the time, Pallas kernels for 0%

commit v1 on v0

--- a/solution.py
+++ b/solution.py
@@ -1,12 +1,22 @@
+import functools
 import jax
 import jax.numpy as jnp
 from jax import lax
 from jax.sharding import PartitionSpec as P
+from jax.lax import psum
 
 BLK = 128
 WIN = 1
 TILES = 2
 NORM_EPS = 1e-06
+
+
+def part_the_targets(w_in, axis_name, peer_axis):
+    z2 = psum(w_in, axis_name)
+    return psum(z2, peer_axis)
+
+
+derive_stocks_here = functools.partial(part_the_targets, axis_name="song", peer_axis="seq")
 
 
 def extended_2(block, sides, width):
@@ -190,8 +200,8 @@
     unnormed_lyric_gradient, lyric_gain_vector = norm_back(
         lyric_keys[0], lyric_inv, k_gain, summed_key.reshape(lyric_local, head_count, head_size)
     )
-    total_query_gain, total_key_gain = lax.psum(
-        (query_gain_vector, key_gain_vector + lyric_gain_vector), ("song", "seq")
+    total_query_gain, total_key_gain = derive_stocks_here(
+        (query_gain_vector, key_gain_vector + lyric_gain_vector)
     )
     return (
         output_list.reshape(1, frames, model_width),

time: 656 us -> 737 us (1.12)
  waiting for transfers between devices: 130 us -> 279 us
  blocking collectives: 362 us -> 290 us
    unnamed x4, waiting for transfers between devices: 0.05 us -> 149 us
    psum x1, blocking collectives: 82.4 us -> 8.46 us  [part_the_targets(): z2 = psum(w_in, axis_name)]
    unnamed x66 -> x78, local copies, waits for them, and re-layouts: 21.5 us -> 22.7 us
  transfers between devices with their start and end apart: 7 -> 7, of which waited for: 4 -> 5; matrix products, arithmetic and copies ran while one was open for 16% -> 12% of each run, Pallas kernels for 0% -> 0%
where the time goes in v1:
time: 737 us; the launch traced here: 732 us
  blocking collectives  290 us (39%)
  waiting for transfers between devices  279 us (38%)
  local copies, waits for them, and re-layouts  62.1 us (8%)
  other arithmetic  56.8 us (8%)
  between operations  15.7 us (2%)
  matrix products  15.3 us (2%)
  starting transfers between devices  12.9 us (2%)
    unnamed x1, blocking collectives  281 us
    unnamed x4, waiting for transfers between devices  149 us
    all_gather x1, waiting for transfers between devices, body(): lax.all_gather(lyric_norm.reshape(lyric_local, model_width), 'seq', axis=...  69.1 us
    all_gather x1, waiting for transfers between devices, body(): lax.all_gather(lyric_values[0], 'seq', axis=0, tiled=True)  53.6 us
    unnamed x78, local copies, waits for them, and re-layouts  22.7 us
    scatter-add x1, other arithmetic, body(): lyric_grad_val = jnp.zeros((lyric_total, head_count, head_size), jnp.floa...  20.2 us
    scatter-add x1, other arithmetic, body(): lyric_grad_key = jnp.zeros((lyric_total, head_count, head_size), jnp.floa...  20.2 us
  transfers between devices with their start and end apart: 7, of which 5 were waited for; matrix products, arithmetic and copies ran while one was open for 12% of the time, Pallas kernels for 0%

profile of v1, /device:TPU:1, one launch (start us, length us, event | category | flops | bytes accessed | tf_op | source)
XLA Modules:
  0.0 732.0 jit_solution(5339710191172339671)
XLA Ops:
  7.2 1.4 copy.99
  8.7 0.8 convert_bitcast_fusion
  9.6 0.7 broadcast_bitcast_fusion.2
  10.3 1.4 fusion.41
  11.8 1.3 copy.98
  13.1 1.4 copy.97
  14.5 1.1 multiply_reduce_fusion.2
  15.7 0.4 multiply_convert_fusion.1
  16.1 5.2 collective-permute-start.1
  21.3 1.9 collective-permute-start
  24.1 1.0 copy.107
  25.1 1.2 copy.103
  26.3 0.7 dynamic-slice.30
  27.9 5.7 collective-permute-done.1
  33.5 1.9 collective-permute-done
  35.5 1.7 pad_maximum_fusion
  37.2 1.5 fusion.52
  38.7 1.6 copy.105
  40.3 53.6 %all-gather.5.cloned.1.call-done = bf16[1,384,2048]{2,0,1:T(2,128)(2,1)} async-done(((bf16[1,6,2048]{2,0,1:T(2,128)(2,1)}), bf16[1,384,2048]{2,0,1:T(2,128)(2,1)}) %all-gather.5.cloned.1.call-update) | async-done | bytes 1572880 | tf_op jit(solution)/shard_map/all_gather | solution.py:106
  93.9 6.9 copy.100
  100.9 2.0 copy.101
  102.9 69.1 %all-gather.7.cloned.1.call-done = bf16[64,6,2048]{2,1,0:T(8,128)(2,1)} async-done(((bf16[1,6,2048]{2,1,0:T(8,128)(2,1)}), bf16[64,6,2048]{2,1,0:T(8,128)(2,1)}) %all-gather.7.cloned.1.call-update) | async-done | bytes 1572880 | tf_op jit(solution)/shard_map/all_gather | solution.py:105
  172.0 4.4 reshape.472
  176.4 3.2 gather_fusion.1
  179.5 1.8 gather_fusion
  181.3 1.6 copy.102
  182.9 1.6 copy_select_fusion
  184.7 1.6 fusion.2
  186.3 3.9 fusion.56
  190.2 0.8 copy-done.31
  191.0 2.5 multiply_reduce_fusion
  193.4 2.0 copy.114
  195.5 3.8 fusion
  199.3 0.9 fusion.57
  200.2 0.5 copy-done.18
  201.0 2.7 fusion.18
  203.6 1.1 slice.221
  204.7 1.3 fusion.54
  206.9 1.7 fusion.55
  208.7 2.1 collective-permute-start.3
  210.8 3.6 collective-permute-start.2
  214.6 2.0 copy.112
  216.8 20.2 %scatter_fusion = f32[384,16,128]{2,1,0:T(8,128)S(1)} fusion(f32[384,16,128]{2,1,0:T(8,128)S(1)} %broadcast.403.clone, s32[256]{0:T(256)S(1)} %bitcast.227, f32[256,16,128]{2,1,0:T(8,128)} %copy.112), kind=kCustom, calls=%fused_computation.2 | custom fusion | flops 524288 | bytes 6292480 | tf_op jit(solution)/shard_map/scatter-add | solution.py:144
  237.1 3.0 copy.146
  240.1 1.2 copy-done.2
  241.3 0.3 copy-done.23
  242.0 1.0 copy.115
  243.0 2.4 slice.228
  245.3 1.8 slice_bitcast_fusion
  247.1 2.0 copy.113
  249.3 20.2 %scatter_fusion.1 = f32[384,16,128]{2,1,0:T(8,128)S(1)} fusion(f32[384,16,128]{2,1,0:T(8,128)S(1)} %broadcast.403.clone.1, s32[256]{0:T(256)S(1)} %bitcast.228, f32[256,16,128]{2,1,0:T(8,128)} %copy.113), kind=kCustom, calls=%fused_computation.3 | custom fusion | flops 524288 | bytes 6292480 | tf_op jit(solution)/shard_map/scatter-add | solution.py:149
  269.6 3.1 copy.145
  272.9 1.8 fusion.14
  274.7 1.6 fusion.22
  276.3 0.4 fusion.12
  276.7 1.0 copy.116
  277.7 2.7 fusion.16
  280.4 2.0 copy.117
  282.5 148.9 %all-reduce.7.cloned.1.call-done = f32[384,2048]{1,0:T(8,128)} async-done(((f32[384,2048]{1,0:T(8,128)}), f32[384,2048]{1,0:T(8,128)}) %all-reduce.7.cloned.1.call-update) | async-done | bytes 3145744
  431.4 0.9 dynamic-slice_bitcast_fusion
  432.5 1.6 fusion.33
  434.1 8.5 %all-reduce.3 = (f32[128]{0:T(128)S(1)}, f32[128]{0:T(128)S(1)}) all-reduce(f32[128]{0:T(128)S(1)} %get-tuple-element.214, f32[128]{0:T(128)S(1)} %add.206), channel_id=1, replica_groups=mesh['song'=4,'seq'=64] {'song'}, use_global_device_ids=true, to_apply=%region_13.15 | all-reduce | flops 256 | bytes 2048 | tf_op jit(solution)/shard_map/psum | solution.py:15
  442.5 281.4 %all-reduce.8 = (bf16[384,2048]{1,0:T(8,128)(2,1)}, f32[128]{0:T(128)}, f32[128]{0:T(128)}) all-reduce(f32[384,2048]{1,0:T(8,128)S(1)} %bitcast.202, f32[128]{0:T(128)S(1)} %get-tuple-element.219, f32[128]{0:T(128)S(1)} %get-tuple-element.220), channel_id=4, replica_groups=mesh['song'=4,'seq'=64] {'seq'}, use_global_device_ids=true, to_apply=%region_11.13.clone | all-reduce | flops 786688 | bytes 4720640
  724.0 1.5 fusion.40
  (98 shorter events, 3.3 us)
Async XLA Ops:
  7.2 86.8 %all-gather.5.cloned.1.call-start = ((), (), s32[]{:S(2)}) async-start(), calls=%async_computation | async-start | bytes 3194880 | tf_op jit(solution)/shard_map/all_gather | solution.py:106
  8.7 163.3 %all-gather.7.cloned.1.call-start = ((), (), s32[]{:S(2)}) async-start(), calls=%async_computation.1 | async-start | bytes 2129920 | tf_op jit(solution)/shard_map/all_gather | solution.py:105
  11.7 419.6 %all-reduce.7.cloned.1.call-start = ((), (), s32[]{:S(2)}) async-start(), calls=%async_computation.2 | async-start | bytes 6291456
  13.1 10.8 %copy-start.29 = (s32[1,1,2]{2,1,0:T(1,128)S(1)}, s32[1,1,2]{2,1,0:T(1,128)}, u32[]{:S(2)}) copy-start(s32[1,1,2]{2,1,0:T(1,128)} %param.44) | copy-start | bytes 28
  13.1 10.9 %copy-start.24 = (bf16[1,128,2048]{2,1,0:T(8,128)(2,1)S(1)}, bf16[1,128,2048]{2,1,0:T(8,128)(2,1)}, u32[]{:S(2)}) copy-start(bf16[1,128,2048]{2,1,0:T(8,128)(2,1)} %param.43) | copy-start | bytes 1572868
  14.5 9.5 %copy-start.3 = (bf16[1,128,2048]{1,2,0:T(8,128)(2,1)}, bf16[1,128,2048]{1,2,0:T(8,128)(2,1)S(1)}, u32[]{:S(2)}) copy-start(bf16[1,128,2048]{1,2,0:T(8,128)(2,1)S(1)} %copy.97) | copy-start | bytes 1572868
  15.6 10.7 %copy-start.30 = (u32[256]{0:T(256)S(1)}, u32[256]{0:T(256)}, u32[]{:S(2)}) copy-start(u32[256]{0:T(256)} %constant.274) | copy-start | bytes 3076
  16.0 11.7 %copy-start.28 = (f32[128]{0:T(128)S(1)}, f32[128]{0:T(128)}, u32[]{:S(2)}) copy-start(f32[128]{0:T(128)} %param.41) | copy-start | bytes 1540
  16.1 17.4 %collective-permute-start.1 = (bf16[2,128,2048]{1,2,0:T(8,128)(2,1)S(1)}, bf16[2,128,2048]{1,2,0:T(8,128)(2,1)}, u32[]{:S(2)}, u32[]{:S(2)}) collective-permute-start(bf16[2,128,2048]{1,2,0:T(8,128)(2,1)S(1)} %pad_maximum_fusion.9), channel_id=1, source_target_pairs={{1,0},{2,1},{3,2},{4,3},{5,4},{6,5},{7,6},{8,7},{9,8},{10,9},{11,1... | collective-permute-start | bytes 3145736 | tf_op jit(solution)/shard_map/ppermute | solution.py:30
  21.3 14.2 %collective-permute-start = (bf16[2,128,2048]{1,2,0:T(8,128)(2,1)S(1)}, bf16[2,128,2048]{1,2,0:T(8,128)(2,1)}, u32[]{:S(2)}, u32[]{:S(2)}) collective-permute-start(bf16[2,128,2048]{1,2,0:T(8,128)(2,1)S(1)} %pad_maximum_fusion.9), channel_id=1, source_target_pairs={{0,1},{1,2},{2,3},{3,4},{4,5},{5,6},{6,7},{7,8},{8,9},{9,10},{10,1... | collective-permute-start | bytes 3145736 | tf_op jit(solution)/shard_map/ppermute | solution.py:27
  26.3 173.9 %copy-start.1 = (f32[1,128,2048]{1,2,0:T(8,128)}, f32[1,128,2048]{1,2,0:T(8,128)S(1)}, u32[]{:S(2)}) copy-start(f32[1,128,2048]{1,2,0:T(8,128)S(1)} %copy.103) | copy-start | bytes 3145732
  102.9 76.6 %copy-start.15 = (bf16[384,16,128]{2,1,0:T(8,128)(2,1)S(1)}, bf16[384,16,128]{2,1,0:T(8,128)(2,1)}, u32[]{:S(2)}) copy-start(bf16[384,16,128]{2,1,0:T(8,128)(2,1)} %copy.101) | copy-start | bytes 4718596
  182.9 1.8 copy-start.17
  184.5 1.7 copy-start.20
  184.7 5.5 copy-start.22
  184.7 1.6 copy-start.25
  186.3 4.7 copy-start.31
  186.3 4.7 copy-start.19
  199.3 1.4 copy-start.18
  199.3 1.7 copy-start.21
  201.0 13.5 %copy-start = (f32[1,640,16,128]{1,3,2,0:T(8,128)}, f32[1,640,16,128]{1,3,2,0:T(8,128)S(1)}, u32[]{:S(2)}) copy-start(f32[1,640,16,128]{1,3,2,0:T(8,128)S(1)} %get-tuple-element.247) | copy-start | bytes 15728644
  206.0 0.8 copy-start.7
  206.0 1.0 copy-start.9
  206.3 2.4 copy-start.11
  206.3 2.4 copy-start.13
  208.7 64.1 %collective-permute-start.3 = (bf16[2,128,2048]{1,2,0:T(8,128)(2,1)}, bf16[2,128,2048]{1,2,0:T(8,128)(2,1)}, u32[]{:S(2)}, u32[]{:S(2)}) collective-permute-start(bf16[2,128,2048]{1,2,0:T(8,128)(2,1)} %get-tuple-element.237), channel_id=1, source_target_pairs={{1,0},{2,1},{3,2},{4,3},{5,4},{6,5},{7,6},{8,7},{9,8},{10,9},{11,1... | collective-permute-start | bytes 3145736 | tf_op jit(solution)/shard_map/ppermute | solution.py:30
  210.8 62.0 %collective-permute-start.2 = (bf16[2,128,2048]{1,2,0:T(8,128)(2,1)}, bf16[2,128,2048]{1,2,0:T(8,128)(2,1)}, u32[]{:S(2)}, u32[]{:S(2)}) collective-permute-start(bf16[2,128,2048]{1,2,0:T(8,128)(2,1)} %get-tuple-element.236), channel_id=1, source_target_pairs={{0,1},{1,2},{2,3},{3,4},{4,5},{5,6},{6,7},{7,8},{8,9},{9,10},{10,1... | collective-permute-start | bytes 3145736 | tf_op jit(solution)/shard_map/ppermute | solution.py:27
  240.1 1.2 copy-start.2
  240.1 1.5 copy-start.23
  269.6 3.2 copy-start.4
  269.6 3.2 copy-start.6
  269.6 3.2 copy-start.8
  269.6 3.2 copy-start.10
  269.6 3.2 copy-start.12
  269.6 3.2 copy-start.14
  272.8 1.9 copy-start.16
  272.8 1.9 copy-start.27
  277.7 154.7 %copy-start.26 = (bf16[1,6,2048]{2,1,0:T(8,128)(2,1)S(1)}, bf16[1,6,2048]{2,1,0:T(8,128)(2,1)}, u32[]{:S(2)}) copy-start(bf16[1,6,2048]{2,1,0:T(8,128)(2,1)} %param.39) | copy-start | bytes 73732
  277.7 164.8 %copy-start.5 = (f32[48,8,16,128]{3,1,2,0:T(8,128)S(1)}, f32[48,8,16,128]{3,1,2,0:T(8,128)}, u32[]{:S(2)}) copy-start(f32[48,8,16,128]{3,1,2,0:T(8,128)} %copy.145) | copy-start | bytes 9437188
Sparse Core Ops, SparseCore 0:
  11.3 82.5 all-gather.4
  97.3 74.6 all-gather.6
  240.2 191.0 all-reduce.6
